TPU v7x, 128 devices: a whole 4x4x4 slice. The times are simulated.
128 devices in a mesh: ctx: 16 (over y, x), tp: 8 (over z, core).
Axes of the slice: x: 4, y: 4, z: 4, core: 2. Of those that a mesh axis runs over, the one named last changes fastest.
Arguments:
- ssm_input: bfloat16 [4096, 8192], P('ctx', 'tp'), may hold values from -6 to 6
- dt_raw: float32 [4096, 128], P('ctx', 'tp'), may hold values from -5 to 5
- b_proj: bfloat16 [4096, 8, 256], P('ctx', 'tp'), may hold values from -0.59765625 to 0.59765625
- c_proj: bfloat16 [4096, 8, 256], P('ctx', 'tp'), may hold values from -0.59765625 to 0.59765625
- dt_bias: float32 [128], P('tp'), may hold values from -1.5 to 0.5
- decay_rate: float32 [128], P('tp'), may hold values from 0.0002 to 0.05
- skip_gain: float32 [128], P('tp'), may hold values from 0.5 to 1.5
- doc_start: int32 [4096], P('ctx'), may hold values 0 or 1
- out_weight: bfloat16 [8192, 8192], P('tp'), may hold values from -0.0625 to 0.0625
- grad_out: bfloat16 [4096, 8192], P(('ctx', 'tp')), may hold values from -6 to 6
Outputs:
- layer_out: bfloat16 [4096, 8192], P(('ctx', 'tp'))
- grad_input: bfloat16 [4096, 8192], P('ctx', 'tp')
- grad_dt: float32 [4096, 128], P('ctx', 'tp')
- grad_b: bfloat16 [4096, 8, 256], P('ctx', 'tp')
- grad_c: bfloat16 [4096, 8, 256], P('ctx', 'tp')
- weight_grad: bfloat16 [8192, 8192], P('ctx', 'tp')
Inputs may be any that keep to these rules, and one draw needn't show every extreme that they name: `doc_start`: 1 marks the first token of a document; a document runs on until the next 1, across slabs.
All inputs are finite; a program needn't handle non-finite values. No bound on the sum of `doc_start` on one device may be relied on, other than what follows from the above.
Results may differ from a plain program's by a relative error of at most 0.022.
Values may be sent and summed in bfloat16 or wider, within the bound.
No kernel may reach another device: no remote copies, remote signals or barrier semaphores. Data moves between devices by JAX's collectives and lax.ppermute only.
A program may use at most 256 MiB of HBM per device.

v0:
```python
import jax
import jax.numpy as jnp
from jax import lax
from jax.sharding import PartitionSpec as P

HIGHEST = lax.Precision.HIGHEST


def prefix(value, axis, combine, identity, reverse):
    devices, mine = (lax.axis_size(axis), lax.axis_index(axis))
    everything = jax.tree.map(
        lambda part, kind: lax.all_gather(part.astype(kind), axis),
        value,
        (jnp.bfloat16, jnp.bfloat16),
    )
    start = jax.tree.map(
        lambda part, zero: jnp.broadcast_to(jnp.asarray(zero, part.dtype), part.shape),
        value,
        identity,
    )

    def step(k, before):
        at = devices - 1 - k if reverse else k
        reached = at > mine if reverse else at < mine
        new = combine(
            before, jax.tree.map(lambda part, own: part[at].astype(own.dtype), everything, value)
        )
        return jax.tree.map(lambda a, b: jnp.where(reached, a, b), new, before)

    return lax.fori_loop(0, devices, step, start)


def block_ssd(
    seq_in, step_raw, b_rows, c_rows, scores, carried, doc_start, bias_heads, rate_heads, skip_heads
):
    length = seq_in.shape[0]
    step_size = jax.nn.softplus(step_raw + bias_heads)
    cumul = jnp.cumsum(-step_size * rate_heads, axis=0)
    segment = jnp.cumsum(doc_start)
    reach = (segment == 0).astype(jnp.float32)
    order = jnp.arange(length)
    causal = (segment[:, None] == segment[None, :]) & (order[:, None] >= order[None, :])
    cum_heads = jnp.transpose(cumul, (1, 2, 0))
    differ = cum_heads[:, :, :, None] - cum_heads[:, :, None, :]
    decays = jnp.exp(jnp.where(causal, differ, -jnp.inf))
    mixing = decays * scores[:, None] * jnp.transpose(step_size, (1, 2, 0))[:, :, None, :]
    inside = jnp.einsum("gkts,sgkp->tgkp", mixing, seq_in, precision=HIGHEST)
    entry = jnp.exp(cumul) * reach[:, None, None]
    from_carry = entry[..., None] * jnp.einsum("tgn,gkpn->tgkp", c_rows, carried, precision=HIGHEST)
    mixer = inside + from_carry + skip_heads[..., None] * seq_in
    same_last = (segment == segment[-1]).astype(jnp.float32)
    tail = jnp.exp(cumul[-1] - cumul) * same_last[:, None, None] * step_size
    local_state = jnp.einsum("sgk,sgkp,sgn->gkpn", tail, seq_in, b_rows, precision=HIGHEST)
    through = reach[-1] * jnp.exp(cumul[-1])
    return (mixer, local_state, through)


def chain_combine(earlier, later):
    return (earlier[0] * later[0], later[0][..., None, None] * earlier[1] + later[1])


def shards(
    ssm_input,
    dt_raw,
    b_proj,
    c_proj,
    dt_bias,
    decay_rate,
    skip_gain,
    doc_start,
    out_weight,
    grad_out,
):
    rows = ssm_input.shape[0]
    heads = dt_raw.shape[1]
    head_dim = ssm_input.shape[1] // heads
    seq_f32 = ssm_input.astype(jnp.float32).reshape(rows, 1, heads, head_dim)
    step_raw = dt_raw.reshape(rows, 1, heads)
    b_rows = b_proj.astype(jnp.float32)
    c_rows = c_proj.astype(jnp.float32)
    bias_heads = dt_bias.reshape(1, heads)
    rate_heads = decay_rate.reshape(1, heads)
    skip_heads = skip_gain.reshape(1, heads)
    scores = jnp.einsum("tgn,sgn->gts", c_proj, b_proj, preferred_element_type=jnp.float32)
    step_size = jax.nn.softplus(step_raw + bias_heads)
    cumul = jnp.cumsum(-step_size * rate_heads, axis=0)
    segment = jnp.cumsum(doc_start)
    reach = (segment == 0).astype(jnp.float32)
    same_last = (segment == segment[-1]).astype(jnp.float32)
    tail = jnp.exp(cumul[-1] - cumul) * same_last[:, None, None] * step_size
    local_state = jnp.einsum("sgk,sgkp,sgn->gkpn", tail, seq_f32, b_rows, precision=HIGHEST)
    through = reach[-1] * jnp.exp(cumul[-1])
    identity_pair = (jnp.ones_like(through), jnp.zeros_like(local_state))
    carried = prefix((through, local_state), "ctx", chain_combine, identity_pair, False)[1]

    def local_fn(seq_arg, step_arg, b_arg, c_arg, score_arg):
        return block_ssd(
            seq_arg,
            step_arg,
            b_arg,
            c_arg,
            score_arg,
            carried,
            doc_start,
            bias_heads,
            rate_heads,
            skip_heads,
        )

    (mixer, _, _), pullback = jax.vjp(local_fn, seq_f32, step_raw, b_rows, c_rows, scores)
    mixer_bf = mixer.reshape(rows, heads * head_dim).astype(jnp.bfloat16)
    layer_out = lax.psum_scatter(
        jnp.dot(mixer_bf, out_weight, preferred_element_type=jnp.float32).astype(jnp.bfloat16),
        "tp",
        scatter_dimension=0,
        tiled=True,
    )
    grad_full = lax.all_gather(grad_out, "tp", axis=0, tiled=True)
    grad_mix = lax.dot_general(
        grad_full, out_weight, (((1,), (1,)), ((), ())), preferred_element_type=jnp.float32
    ).astype(jnp.bfloat16)
    grad_heads = grad_mix.astype(jnp.float32).reshape(rows, 1, heads, head_dim)
    entry = jnp.exp(cumul) * reach[:, None, None]
    local_grad = jnp.einsum("tgk,tgkp,tgn->gkpn", entry, grad_heads, c_rows, precision=HIGHEST)
    grad_next = prefix((through, local_grad), "ctx", chain_combine, identity_pair, True)[1]
    through_grad = jnp.sum(grad_next * carried, axis=(2, 3))
    grad_seq, grad_step, grad_brows, grad_crows, grad_scores = pullback(
        (grad_heads, grad_next, through_grad)
    )
    grad_brows = grad_brows + jnp.einsum("gts,tgn->sgn", grad_scores, c_rows, precision=HIGHEST)
    grad_crows = grad_crows + jnp.einsum("gts,sgn->tgn", grad_scores, b_rows, precision=HIGHEST)
    weight_sum = lax.psum_scatter(
        lax.dot_general(
            grad_full, mixer_bf, (((0,), (0,)), ((), ())), preferred_element_type=jnp.float32
        ).astype(jnp.bfloat16),
        "ctx",
        scatter_dimension=0,
        tiled=True,
    )
    return (
        layer_out,
        grad_seq.reshape(rows, heads * head_dim).astype(jnp.bfloat16),
        grad_step.reshape(rows, heads),
        grad_brows.astype(jnp.bfloat16),
        grad_crows.astype(jnp.bfloat16),
        weight_sum,
    )


def solution(mesh):
    in_specs = (
        P("ctx", "tp"),
        P("ctx", "tp"),
        P("ctx", "tp", None),
        P("ctx", "tp", None),
        P("tp"),
        P("tp"),
        P("tp"),
        P("ctx"),
        P("tp", None),
        P(("ctx", "tp"), None),
    )
    out_specs = (
        P(("ctx", "tp"), None),
        P("ctx", "tp"),
        P("ctx", "tp"),
        P("ctx", "tp", None),
        P("ctx", "tp", None),
        P("ctx", "tp"),
    )
    return jax.shard_map(shards, mesh=mesh, in_specs=in_specs, out_specs=out_specs, check_vma=False)
```

profile of v0, /device:TPU:0, one launch (start us, length us, event | category | flops | bytes accessed | tf_op | source)
XLA Modules:
  0.0 452.5 jit_solution(1089252134521595264)
XLA Ops:
  12.2 32.3 %all-gather.6.cloned.1.call-done = bf16[256,8192]{1,0:T(8,128)(2,1)} async-done(((bf16[32,8192]{1,0:T(8,128)(2,1)}), bf16[256,8192]{1,0:T(8,128)(2,1)}) %all-gather.6.cloned.1.call-update) | async-done | bytes 4194320 | tf_op jit(solution)/shard_map/all_gather | solution.py:118
  44.6 11.6 %convolution_convert_fusion.3 = bf16[256,1024]{1,0:T(8,128)(2,1)S(1)} fusion(bf16[256,8192]{1,0:T(8,128)(2,1)} %all-gather.6.cloned.1.call-done, bf16[1024,8192]{1,0:T(8,128)(2,1)} %param.22), kind=kOutput, calls=%fused_computation.43 | convolution fusion | flops 4295229440 | bytes 21495808 | tf_op jit(solution)/shard_map/dot_general | solution.py:119
  56.4 1.4 convolution_convert_fusion.1
  60.6 22.2 %all_gather.21 = bf16[16,1,16]{2,1,0:T(2,128)(2,1)} all-gather(bf16[1,1,16]{2,1,0:T(2,128)(2,1)S(1)} %get-tuple-element.399), channel_id=1, replica_groups=mesh['ctx'=16,'tp'=8] {'ctx'}, dimensions={0}, use_global_device_ids=true | all-gather | bytes 544 | tf_op jit(solution)/shard_map/all_gather | solution.py:12
  82.8 1.9 compare_convert_fusion
  84.7 43.8 %all-gather.10.cloned.1.call-done = bf16[256,64,256]{2,1,0:T(8,128)(2,1)} async-done(((bf16[16,64,256]{2,1,0:T(8,128)(2,1)}), bf16[256,64,256]{2,1,0:T(8,128)(2,1)}) %all-gather.10.cloned.1.call-update) | async-done | bytes 8388624 | tf_op jit(solution)/shard_map/all_gather | solution.py:12
  128.5 31.4 %while.31 = (s32[]{:T(128)}, f32[1,16,64,256]{3,2,1,0:T(8,128)S(1)}, s32[]{:T(128)}, bf16[16,1,16]{2,1,0:T(2,128)(2,1)}, bf16[16,1,16,64,256]{4,3,2,1,0:T(8,128)...) while((s32[]{:T(128)}, f32[1,16,64,256]{3,2,1,0:T(8,128)S(1)}, s32[]{:T(128)}, ...), condition=%wide.region_8.9_spmd.clone, body=%wide.region_7.8_spmd.clone.sunk | while | flops 1310744 | bytes 2621775 | solution.py:30
  129.2 1.3 fusion.99
  148.7 1.3 fusion.99
  150.6 1.3 fusion.99
  154.6 1.3 fusion.99
  159.9 2.2 fusion.50
  162.1 1.5 copy.170
  163.5 1.6 multiply_multiply_fusion
  165.8 1.7 multiply_reduce_fusion.4
  168.2 1.4 fusion.75
  169.7 1.6 copy.146
  171.2 2.2 convolution_convert_fusion.2
  176.5 1.3 bitcast_add_fusion.2
  177.8 1.5 fusion.62
  180.2 1.6 copy.140
  181.8 62.1 %all-gather.8.cloned.1.call-done = bf16[256,64,256]{2,1,0:T(8,128)(2,1)} async-done(((bf16[16,64,256]{2,1,0:T(8,128)(2,1)}), bf16[256,64,256]{2,1,0:T(8,128)(2,1)}) %all-gather.8.cloned.1.call-update) | async-done | bytes 8388624 | tf_op jit(solution)/shard_map/all_gather | solution.py:12
  243.9 31.2 %while.30 = (s32[]{:T(128)}, f32[1,16,64,256]{3,2,1,0:T(8,128)S(1)}, s32[]{:T(128)}, bf16[16,1,16]{2,1,0:T(2,128)(2,1)}, bf16[16,1,16,64,256]{4,3,2,1,0:T(8,128)(2,1)}, /*index=5*/s32[]{:T(128)}, s32[]{:T(128)}) while((s32[]{:T(128)}, f32[1,16,64,256]{3,2,1,0:T(8,128)S(1)}, s32[]{:T(128)}, bf16[16,1,16]{2,1,0:T(2,128)(2,1)}, ...), condition=%wide.region_5.6_spmd.clone, body=%wide.region_4.5_spmd.clone.sunk | while | flops 1310740 | bytes 2621713 | solution.py:30
  244.6 1.3 fusion.98
  260.2 1.3 fusion.98
  264.1 1.3 fusion.98
  276.4 5.8 %fusion.40 = bf16[256,1,16,64]{0,3,2,1:T(8,128)(2,1)} fusion(bf16[256,16,64]{0,2,1:T(8,128)(2,1)} %bitcast.245, f32[16,256]{1,0:T(8,128)} %copy.140, f32[256,256]{1,0:T(8,128)} %fusion.77, f32[16,256]{1,0:T(8,128)} %bitcast_add_fusion.2, pred[256,256]{1,0:T(8,128)(4,1)} %fusion.62, f32[256,1,16,64]{0,3,2,1:T(8,128)} %bitcast.256, ...), kind=kOutput, calls=%fused_computation.42 | convolution fusion | flops 810811392 | bytes 3522624 | tf_op jit(solution)/shard_map/jvp(gkts,sgkp->tgkp)/dot_general | solution.py:47
  282.2 12.6 %convert_bitcast_fusion = bf16[8192,1024]{0,1:T(8,128)(2,1)} fusion(bf16[256,1024]{0,1:T(8,128)(2,1)} %bitcast.248, bf16[256,8192]{1,0:T(8,128)(2,1)} %all-gather.6.cloned.1.call-done), kind=kOutput, calls=%fused_computation.6 | convolution fusion | flops 4303355904 | bytes 21495808 | tf_op jit(solution)/shard_map/dot_general | solution.py:133
  295.1 12.5 %convolution_convert_fusion = bf16[256,8192]{1,0:T(8,128)(2,1)} fusion(bf16[256,1024]{0,1:T(8,128)(2,1)} %bitcast.249, bf16[1024,8192]{1,0:T(8,128)(2,1)} %param.22), kind=kOutput, calls=%fused_computation.7 | convolution fusion | flops 4297064448 | bytes 21495808 | tf_op jit(solution)/shard_map/dot_general | solution.py:113
  307.6 2.1 copy.152
  309.7 5.2 %fusion.37 = bf16[256,1,16,64]{0,3,2,1:T(8,128)(2,1)} fusion(bf16[16,64,256]{2,1,0:T(8,128)(2,1)} %bitcast.260, f32[16,256]{1,0:T(8,128)} %copy.140, f32[256,256]{1,0:T(8,128)} %fusion.77, f32[16,256]{1,0:T(8,128)} %bitcast_add_fusion.2, pred[256,256]{1,0:T(8,128)(4,1)} %fusion.62, f32[256,16,64]{0,2,1:T(8,128)S(1)} %bitcast.242, ...), kind=kOutput, calls=%fused_computation.39 | convolution fusion | flops 810811392 | bytes 3522624 | tf_op jit(solution)/shard_map/transpose(jvp(gkts,sgkp->tgkp))/dot_general | solution.py:47
  314.8 2.0 copy.162
  316.9 5.2 %fusion.9 = (f32[16,256]{1,0:T(8,128)}, f32[16,256]{1,0:T(8,128)}, f32[16,256]{1,0:T(8,128)}, f32[256,256]{1,0:T(8,128)}) fusion(f32[16,256]{1,0:T(8,128)} %copy.140, f32[256,256]{1,0:T(8,128)} %fusion.77, f32[16,256]{1,0:T(8,128)} %bitcast_add_fusion.2, pred[256,256]{1,0:T(8,128)(4,1)} %fusion.62, bf16[16,64,256]{2,1,0:T(8,128)(2,1)} %bitcast.261, ...), kind=kOutput, calls=%fused_computation.17 | convolution fusion | flops 147771392 | bytes 1720320 | tf_op jit(solution)/shard_map/transpose(jvp(gkts,sgkp->tgkp))/dot_general | solution.py:47
  322.1 1.5 copy.156
  323.6 1.5 copy.157
  325.0 1.5 copy.153
  326.5 2.9 fusion.44
  329.4 1.9 fusion.49
  331.3 1.7 copy.164
  333.0 1.9 convolution_bitcast_fusion.2
  335.9 1.5 copy.155
  337.6 1.3 bitcast_multiply_fusion.2
  339.0 1.5 add_add_fusion
  340.5 2.5 reduce-window.29
  345.2 3.4 fusion.47
  348.6 56.6 %reduce-scatter.5.cloned.1.call-done = bf16[512,1024]{0,1:T(8,128)(2,1)} async-done(((bf16[8192,1024]{0,1:T(8,128)(2,1)}), bf16[512,1024]{0,1:T(8,128)(2,1)}) %reduce-scatter.5.cloned.1.call-update) | async-done | bytes 1048592 | tf_op jit(solution)/shard_map/reduce_scatter | solution.py:132
  405.2 2.3 copy.165
  407.4 38.5 %reduce-scatter.3.cloned.1.call-done = bf16[32,8192]{1,0:T(8,128)(2,1)} async-done(((bf16[256,8192]{1,0:T(8,128)(2,1)}), bf16[32,8192]{1,0:T(8,128)(2,1)}) %reduce-scatter.3.cloned.1.call-update) | async-done | bytes 524304 | tf_op jit(solution)/shard_map/reduce_scatter | solution.py:112
  (133 shorter events, 71.0 us)
Async XLA Ops:
  7.2 49.2 %copy-start = (bf16[256,1,256]{2,0,1:T(8,128)(2,1)S(1)}, bf16[256,1,256]{2,0,1:T(8,128)(2,1)}, u32[]{:S(2)}) copy-start(bf16[256,1,256]{2,0,1:T(8,128)(2,1)} %param.17) | copy-start | bytes 393220
  7.2 37.4 %all-gather.6.cloned.1.call-start = ((), (), s32[]{:S(2)}) async-start(), calls=%async_computation.3 | async-start | bytes 4718592 | tf_op jit(solution)/shard_map/all_gather | solution.py:118
  7.9 120.5 %all-gather.10.cloned.1.call-start = ((), (), s32[]{:S(2)}) async-start(), calls=%async_computation.6 | async-start | bytes 8912896 | tf_op jit(solution)/shard_map/all_gather | solution.py:12
  11.8 46.1 %copy-start.12 = (f32[256]{0:T(256)}, f32[256]{0:T(256)S(1)}, u32[]{:S(2)}) copy-start(f32[256]{0:T(256)S(1)} %get-tuple-element.392) | copy-start | bytes 3076
  11.8 46.8 %copy-start.11 = (s32[256]{0:T(256)}, s32[256]{0:T(256)S(1)}, u32[]{:S(2)}) copy-start(s32[256]{0:T(256)S(1)} %get-tuple-element.393) | copy-start | bytes 3076
  11.8 32.8 %copy-start.8 = (f32[16,2,128]{0,2,1:T(8,128)}, f32[16,2,128]{0,2,1:T(8,128)S(1)}, u32[]{:S(2)}) copy-start(f32[16,2,128]{0,2,1:T(8,128)S(1)} %broadcast.148) | copy-start | bytes 49156
  12.2 47.2 %copy-start.5 = (f32[256,1,16]{2,1,0:T(1,128)}, f32[256,1,16]{2,1,0:T(1,128)S(1)}, u32[]{:S(2)}) copy-start(f32[256,1,16]{2,1,0:T(1,128)S(1)} %get-tuple-element.391) | copy-start | bytes 49156
  12.2 44.1 %copy-start.9 = (f32[256,16]{0,1:T(8,128)}, f32[256,16]{0,1:T(8,128)S(1)}, u32[]{:S(2)}) copy-start(f32[256,16]{0,1:T(8,128)S(1)} %copy.144) | copy-start | bytes 49156
  56.1 1.8 copy-start.3
  56.1 3.0 copy-start.2
  57.8 186.1 %all-gather.8.cloned.1.call-start = ((), (), s32[]{:S(2)}) async-start(), calls=%async_computation.5 | async-start | bytes 8912896 | tf_op jit(solution)/shard_map/all_gather | solution.py:12
  59.4 111.9 %copy-start.1 = (bf16[256,1024]{0,1:T(8,128)(2,1)}, bf16[256,1024]{0,1:T(8,128)(2,1)S(1)}, u32[]{:S(2)}) copy-start(bf16[256,1024]{0,1:T(8,128)(2,1)S(1)} %copy.141) | copy-start | bytes 1572868
  128.5 31.4 %copy-start.4 = (bf16[256,1,256]{2,0,1:T(8,128)(2,1)S(1)}, bf16[256,1,256]{2,0,1:T(8,128)(2,1)}, u32[]{:S(2)}) copy-start(bf16[256,1,256]{2,0,1:T(8,128)(2,1)} %param.16) | copy-start | bytes 393220
  165.2 0.6 copy-start.7
  167.6 0.6 copy-start.6
  173.4 231.7 %reduce-scatter.5.cloned.1.call-start = ((), (), s32[]{:S(2)}) async-start(), calls=%async_computation.4 | async-start | bytes 17825792 | tf_op jit(solution)/shard_map/reduce_scatter | solution.py:132
  243.9 32.5 %copy-start.10 = (f32[256,16]{0,1:T(8,128)S(1)}, f32[256,16]{0,1:T(8,128)}, u32[]{:S(2)}) copy-start(f32[256,16]{0,1:T(8,128)} %copy-done.9) | copy-start | bytes 49156
  294.8 151.1 %reduce-scatter.3.cloned.1.call-start = ((), (), s32[]{:S(2)}) async-start(), calls=%async_computation.2 | async-start | bytes 4718592 | tf_op jit(solution)/shard_map/reduce_scatter | solution.py:112
Sparse Core Ops, SparseCore 0:
  9.7 34.7 all-gather.5
  58.0 70.4 all-gather.9
  173.6 70.3 all-gather.7
  295.0 110.1 reduce-scatter.4
  408.0 37.8 reduce-scatter.2
where the time goes:
time: 455 us; the launch traced here: 452 us
  waiting for transfers between devices  234 us (51%)
  other arithmetic  83.1 us (18%)
  matrix products  71 us (16%)
  local copies, waits for them, and re-layouts  26.8 us (6%)
  blocking collectives  22.2 us (5%)
  between operations  14 us (3%)
    all_gather x2, waiting for transfers between devices, prefix(): lax.all_gather(part.astype(kind), axis)  106 us
    reduce_scatter x1, waiting for transfers between devices, shards(): lax.psum_scatter(lax.dot_general(grad_full, mixer_bf, (((0,), (0,)), ((),...  56.6 us
    select_n x32, other arithmetic, step(): return jax.tree.map(lambda a, b: jnp.where(reached, a, b), new, before)  41.2 us
    reduce_scatter x1, waiting for transfers between devices, shards(): lax.psum_scatter(jnp.dot(mixer_bf, out_weight, preferred_element_type=jnp...  38.5 us
    all_gather x1, waiting for transfers between devices, shards(): grad_full = lax.all_gather(grad_out, 'tp', axis=0, tiled=True)  32.3 us
    all_gather x1, blocking collectives, prefix(): lax.all_gather(part.astype(kind), axis)  22.2 us
    convert_element_type x32, other arithmetic, step(): part[at].astype(own.dtype)  20.5 us
    dot_general x3, matrix products, block_ssd(): inside = jnp.einsum('gkts,sgkp->tgkp', mixing, seq_in, precision=HIGHEST)  16.2 us
  transfers between devices with their start and end apart: 5, of which 5 were waited for; matrix products, arithmetic and copies ran while one was open for 16% of the time, Pallas kernels for 0%

commit v1 on v0

--- a/solution.py
+++ b/solution.py
@@ -115,7 +115,10 @@
         scatter_dimension=0,
         tiled=True,
     )
-    grad_full = lax.all_gather(grad_out, "tp", axis=0, tiled=True)
+    n_dev = lax.axis_size("tp")
+    shards_2 = jnp.stack([grad_out for _ in range(n_dev)])
+    shards_2 = lax.all_to_all(shards_2, "tp", split_axis=0, concat_axis=0)
+    grad_full = jnp.concatenate(shards_2, axis=0)
     grad_mix = lax.dot_general(
         grad_full, out_weight, (((1,), (1,)), ((), ())), preferred_element_type=jnp.float32
     ).astype(jnp.bfloat16)

time: 455 us -> 477 us (1.048)
  waiting for transfers between devices: 234 us -> 247 us
  starting transfers between devices: 0.6 us -> 6.1 us
    all_to_all x0 -> x1, waiting for transfers between devices: none -> 46.9 us  [shards(): shards_2 = lax.all_to_all(shards_2, 'tp', split_axis=0, concat_axis=0)]
    all_gather x1 -> x0, waiting for transfers between devices: 32.3 us -> none  [shards(): grad_full = lax.all_gather(grad_out, 'tp', axis=0, tiled=True)]
    all_to_all x0 -> x1, starting transfers between devices: none -> 5.54 us  [shards(): shards_2 = lax.all_to_all(shards_2, 'tp', split_axis=0, concat_axis=0)]
  transfers between devices with their start and end apart: 5 -> 5, of which waited for: 5 -> 5; matrix products, arithmetic and copies ran while one was open for 16% -> 15% of each run, Pallas kernels for 0% -> 0%
where the time goes in v1:
time: 477 us; the launch traced here: 474 us
  waiting for transfers between devices  247 us (52%)
  other arithmetic  82.3 us (17%)
  matrix products  71 us (15%)
  local copies, waits for them, and re-layouts  30.2 us (6%)
  blocking collectives  22.5 us (5%)
  between operations  14 us (3%)
  starting transfers between devices  6.1 us (1%)
    all_gather x2, waiting for transfers between devices, prefix(): lax.all_gather(part.astype(kind), axis)  105 us
    reduce_scatter x1, waiting for transfers between devices, shards(): lax.psum_scatter(lax.dot_general(grad_full, mixer_bf, (((0,), (0,)), ((),...  56.6 us
    all_to_all x1, waiting for transfers between devices, shards(): shards_2 = lax.all_to_all(shards_2, 'tp', split_axis=0, concat_axis=0)  46.9 us
    select_n x32, other arithmetic, step(): return jax.tree.map(lambda a, b: jnp.where(reached, a, b), new, before)  41.2 us
    reduce_scatter x1, waiting for transfers between devices, shards(): lax.psum_scatter(jnp.dot(mixer_bf, out_weight, preferred_element_type=jnp...  38.5 us
    all_gather x1, blocking collectives, prefix(): lax.all_gather(part.astype(kind), axis)  22.5 us
    convert_element_type x32, other arithmetic, step(): part[at].astype(own.dtype)  20.5 us
    dot_general x3, matrix products, block_ssd(): inside = jnp.einsum('gkts,sgkp->tgkp', mixing, seq_in, precision=HIGHEST)  16.2 us
  transfers between devices with their start and end apart: 5, of which 5 were waited for; matrix products, arithmetic and copies ran while one was open for 15% of the time, Pallas kernels for 0%

profile of v1, /device:TPU:0, one launch (start us, length us, event | category | flops | bytes accessed | tf_op | source)
XLA Modules:
  0.0 473.7 jit_solution(8474673955386111068)
XLA Ops:
  7.2 3.5 stack.2
  10.7 5.5 %all-to-all-start = ((bf16[8,32,8192]{2,1,0:T(8,128)(2,1)}), bf16[8,32,8192]{2,1,0:T(8,128)(2,1)}, u32[]{:S(2)}, u32[]{:S(2)}) async-start(bf16[8,32,8192]{2,1,0:T(8,128)(2,1)} %stack.2), calls=%async_computation.1 | async-start | bytes 8388608 | tf_op jit(solution)/shard_map/all_to_all | solution.py:120
  19.1 46.9 %all-to-all-done = bf16[8,32,8192]{2,1,0:T(8,128)(2,1)} async-done(((bf16[8,32,8192]{2,1,0:T(8,128)(2,1)}), bf16[8,32,8192]{2,1,0:T(8,128)(2,1)}, u32[]{:S(2)}, u32[]{:S(2)}) %all-to-all-start) | async-done | bytes 4194336 | tf_op jit(solution)/shard_map/all_to_all | solution.py:120
  66.0 11.6 %convolution_convert_fusion.3 = bf16[256,1024]{1,0:T(8,128)(2,1)S(1)} fusion(bf16[256,8192]{1,0:T(8,128)(2,1)} %bitcast.34, bf16[1024,8192]{1,0:T(8,128)(2,1)} %param.22), kind=kOutput, calls=%fused_computation.43 | convolution fusion | flops 4295229440 | bytes 21495808 | tf_op jit(solution)/shard_map/dot_general | solution.py:122
  77.8 1.4 convolution_convert_fusion.1
  82.7 22.5 %all_gather.18 = bf16[16,1,16]{2,1,0:T(2,128)(2,1)} all-gather(bf16[1,1,16]{2,1,0:T(2,128)(2,1)S(1)} %get-tuple-element.399), channel_id=1, replica_groups=mesh['ctx'=16,'tp'=8] {'ctx'}, dimensions={0}, use_global_device_ids=true | all-gather | bytes 544 | tf_op jit(solution)/shard_map/all_gather | solution.py:12
  105.2 1.9 compare_convert_fusion
  107.1 42.5 %all-gather.7.cloned.1.call-done = bf16[256,64,256]{2,1,0:T(8,128)(2,1)} async-done(((bf16[16,64,256]{2,1,0:T(8,128)(2,1)}), bf16[256,64,256]{2,1,0:T(8,128)(2,1)}) %all-gather.7.cloned.1.call-update) | async-done | bytes 8388624 | tf_op jit(solution)/shard_map/all_gather | solution.py:12
  149.7 31.4 %while.31 = (s32[]{:T(128)}, f32[1,16,64,256]{3,2,1,0:T(8,128)S(1)}, s32[]{:T(128)}, bf16[16,1,16]{2,1,0:T(2,128)(2,1)}, bf16[16,1,16,64,256]{4,3,2,1,0:T(8,128)...) while((s32[]{:T(128)}, f32[1,16,64,256]{3,2,1,0:T(8,128)S(1)}, s32[]{:T(128)}, ...), condition=%wide.region_8.9_spmd.clone, body=%wide.region_7.8_spmd.clone.sunk | while | flops 1310744 | bytes 2621775 | solution.py:30
  158.2 1.3 fusion.99
  169.9 1.3 fusion.99
  181.1 2.2 fusion.50
  183.3 1.5 copy.170
  184.7 1.6 multiply_multiply_fusion
  187.0 1.7 multiply_reduce_fusion.4
  189.4 1.4 fusion.75
  190.9 1.6 copy.146
  192.4 2.2 convolution_convert_fusion.2
  197.7 1.3 bitcast_add_fusion.2
  199.0 1.5 fusion.62
  201.4 1.6 copy.140
  203.0 62.1 %all-gather.5.cloned.1.call-done = bf16[256,64,256]{2,1,0:T(8,128)(2,1)} async-done(((bf16[16,64,256]{2,1,0:T(8,128)(2,1)}), bf16[256,64,256]{2,1,0:T(8,128)(2,1)}) %all-gather.5.cloned.1.call-update) | async-done | bytes 8388624 | tf_op jit(solution)/shard_map/all_gather | solution.py:12
  265.1 31.2 %while.30 = (s32[]{:T(128)}, f32[1,16,64,256]{3,2,1,0:T(8,128)S(1)}, s32[]{:T(128)}, bf16[16,1,16]{2,1,0:T(2,128)(2,1)}, bf16[16,1,16,64,256]{4,3,2,1,0:T(8,128)(2,1)}, /*index=5*/s32[]{:T(128)}, s32[]{:T(128)}) while((s32[]{:T(128)}, f32[1,16,64,256]{3,2,1,0:T(8,128)S(1)}, s32[]{:T(128)}, bf16[16,1,16]{2,1,0:T(2,128)(2,1)}, ...), condition=%wide.region_5.6_spmd.clone, body=%wide.region_4.5_spmd.clone.sunk | while | flops 1310740 | bytes 2621713 | solution.py:30
  269.7 1.3 fusion.98
  271.7 1.3 fusion.98
  273.6 1.3 fusion.98
  297.6 5.8 %fusion.40 = bf16[256,1,16,64]{0,3,2,1:T(8,128)(2,1)} fusion(bf16[256,16,64]{0,2,1:T(8,128)(2,1)} %bitcast.246, f32[16,256]{1,0:T(8,128)} %copy.140, f32[256,256]{1,0:T(8,128)} %fusion.77, f32[16,256]{1,0:T(8,128)} %bitcast_add_fusion.2, pred[256,256]{1,0:T(8,128)(4,1)} %fusion.62, f32[256,1,16,64]{0,3,2,1:T(8,128)} %bitcast.257, ...), kind=kOutput, calls=%fused_computation.42 | convolution fusion | flops 810811392 | bytes 3522624 | tf_op jit(solution)/shard_map/jvp(gkts,sgkp->tgkp)/dot_general | solution.py:47
  303.4 12.6 %convert_bitcast_fusion = bf16[8192,1024]{0,1:T(8,128)(2,1)} fusion(bf16[256,1024]{0,1:T(8,128)(2,1)} %bitcast.249, bf16[256,8192]{1,0:T(8,128)(2,1)} %bitcast.34), kind=kOutput, calls=%fused_computation.6 | convolution fusion | flops 4303355904 | bytes 21495808 | tf_op jit(solution)/shard_map/dot_general | solution.py:136
  316.3 12.5 %convolution_convert_fusion = bf16[256,8192]{1,0:T(8,128)(2,1)} fusion(bf16[256,1024]{0,1:T(8,128)(2,1)} %bitcast.250, bf16[1024,8192]{1,0:T(8,128)(2,1)} %param.22), kind=kOutput, calls=%fused_computation.7 | convolution fusion | flops 4297064448 | bytes 21495808 | tf_op jit(solution)/shard_map/dot_general | solution.py:113
  328.8 2.1 copy.152
  330.9 5.2 %fusion.37 = bf16[256,1,16,64]{0,3,2,1:T(8,128)(2,1)} fusion(bf16[16,64,256]{2,1,0:T(8,128)(2,1)} %bitcast.261, f32[16,256]{1,0:T(8,128)} %copy.140, f32[256,256]{1,0:T(8,128)} %fusion.77, f32[16,256]{1,0:T(8,128)} %bitcast_add_fusion.2, pred[256,256]{1,0:T(8,128)(4,1)} %fusion.62, f32[256,16,64]{0,2,1:T(8,128)S(1)} %bitcast.243, ...), kind=kOutput, calls=%fused_computation.39 | convolution fusion | flops 810811392 | bytes 3522624 | tf_op jit(solution)/shard_map/transpose(jvp(gkts,sgkp->tgkp))/dot_general | solution.py:47
  336.0 2.0 copy.162
  338.1 5.2 %fusion.9 = (f32[16,256]{1,0:T(8,128)}, f32[16,256]{1,0:T(8,128)}, f32[16,256]{1,0:T(8,128)}, f32[256,256]{1,0:T(8,128)}) fusion(f32[16,256]{1,0:T(8,128)} %copy.140, f32[256,256]{1,0:T(8,128)} %fusion.77, f32[16,256]{1,0:T(8,128)} %bitcast_add_fusion.2, pred[256,256]{1,0:T(8,128)(4,1)} %fusion.62, bf16[16,64,256]{2,1,0:T(8,128)(2,1)} %bitcast.262, ...), kind=kOutput, calls=%fused_computation.17 | convolution fusion | flops 147771392 | bytes 1720320 | tf_op jit(solution)/shard_map/transpose(jvp(gkts,sgkp->tgkp))/dot_general | solution.py:47
  343.3 1.5 copy.156
  344.8 1.5 copy.157
  346.2 1.5 copy.153
  347.7 2.9 fusion.44
  350.6 1.9 fusion.49
  352.5 1.7 copy.164
  354.2 1.9 convolution_bitcast_fusion.2
  357.1 1.5 copy.155
  358.8 1.4 bitcast_multiply_fusion.2
  360.1 1.5 add_add_fusion
  361.7 2.5 reduce-window.29
  366.3 3.5 fusion.47
  369.8 56.6 %reduce-scatter.5.cloned.1.call-done = bf16[512,1024]{0,1:T(8,128)(2,1)} async-done(((bf16[8192,1024]{0,1:T(8,128)(2,1)}), bf16[512,1024]{0,1:T(8,128)(2,1)}) %reduce-scatter.5.cloned.1.call-update) | async-done | bytes 1048592 | tf_op jit(solution)/shard_map/reduce_scatter | solution.py:135
  426.4 2.3 copy.165
  428.7 38.5 %reduce-scatter.3.cloned.1.call-done = bf16[32,8192]{1,0:T(8,128)(2,1)} async-done(((bf16[256,8192]{1,0:T(8,128)(2,1)}), bf16[32,8192]{1,0:T(8,128)(2,1)}) %reduce-scatter.3.cloned.1.call-update) | async-done | bytes 524304 | tf_op jit(solution)/shard_map/reduce_scatter | solution.py:112
  (139 shorter events, 72.0 us)
Async XLA Ops:
  7.2 70.7 %copy-start = (bf16[256,1,256]{2,0,1:T(8,128)(2,1)S(1)}, bf16[256,1,256]{2,0,1:T(8,128)(2,1)}, u32[]{:S(2)}) copy-start(bf16[256,1,256]{2,0,1:T(8,128)(2,1)} %param.17) | copy-start | bytes 393220
  10.7 5.6 %copy-start.15 = (s32[256]{0:T(256)S(1)}, s32[256]{0:T(256)}, u32[]{:S(2)}) copy-start(s32[256]{0:T(256)} %param.21) | copy-start | bytes 3076
  10.7 6.0 %copy-start.11 = (f32[256,16]{0,1:T(8,128)S(1)}, f32[256,16]{0,1:T(8,128)}, u32[]{:S(2)}) copy-start(f32[256,16]{0,1:T(8,128)} %param.15) | copy-start | bytes 49156
  10.7 6.1 %copy-start.13 = (f32[16]{0:T(128)S(1)}, f32[16]{0:T(128)}, u32[]{:S(2)}) copy-start(f32[16]{0:T(128)} %param.18) | copy-start | bytes 196
  10.7 6.1 %copy-start.14 = (f32[16]{0:T(128)S(1)}, f32[16]{0:T(128)}, u32[]{:S(2)}) copy-start(f32[16]{0:T(128)} %param.19) | copy-start | bytes 196
  10.7 55.3 %all-to-all-start = ((bf16[8,32,8192]{2,1,0:T(8,128)(2,1)}), bf16[8,32,8192]{2,1,0:T(8,128)(2,1)}, u32[]{:S(2)}, u32[]{:S(2)}) async-start(bf16[8,32,8192]{2,1,0:T(8,128)(2,1)} %stack.2), calls=%async_computation.1 | async-start | bytes 8388608 | tf_op jit(solution)/shard_map/all_to_all | solution.py:120
  16.2 133.4 %all-gather.7.cloned.1.call-start = ((), (), s32[]{:S(2)}) async-start(), calls=%async_computation.6 | async-start | bytes 8912896 | tf_op jit(solution)/shard_map/all_gather | solution.py:12
  18.7 60.7 %copy-start.12 = (f32[256]{0:T(256)}, f32[256]{0:T(256)S(1)}, u32[]{:S(2)}) copy-start(f32[256]{0:T(256)S(1)} %get-tuple-element.392) | copy-start | bytes 3076
  18.7 47.3 %copy-start.8 = (f32[16,2,128]{0,2,1:T(8,128)}, f32[16,2,128]{0,2,1:T(8,128)S(1)}, u32[]{:S(2)}) copy-start(f32[16,2,128]{0,2,1:T(8,128)S(1)} %broadcast.150) | copy-start | bytes 49156
  19.0 62.5 %copy-start.5 = (f32[256,1,16]{2,1,0:T(1,128)}, f32[256,1,16]{2,1,0:T(1,128)S(1)}, u32[]{:S(2)}) copy-start(f32[256,1,16]{2,1,0:T(1,128)S(1)} %get-tuple-element.391) | copy-start | bytes 49156
  19.1 58.7 %copy-start.9 = (f32[256,16]{0,1:T(8,128)}, f32[256,16]{0,1:T(8,128)S(1)}, u32[]{:S(2)}) copy-start(f32[256,16]{0,1:T(8,128)S(1)} %copy.144) | copy-start | bytes 49156
  77.6 2.4 copy-start.3
  77.6 3.7 copy-start.2
  79.3 185.8 %all-gather.5.cloned.1.call-start = ((), (), s32[]{:S(2)}) async-start(), calls=%async_computation.5 | async-start | bytes 8912896 | tf_op jit(solution)/shard_map/all_gather | solution.py:12
  81.5 111.0 %copy-start.1 = (bf16[256,1024]{0,1:T(8,128)(2,1)}, bf16[256,1024]{0,1:T(8,128)(2,1)S(1)}, u32[]{:S(2)}) copy-start(bf16[256,1024]{0,1:T(8,128)(2,1)S(1)} %copy.141) | copy-start | bytes 1572868
  149.7 31.4 %copy-start.4 = (bf16[256,1,256]{2,0,1:T(8,128)(2,1)S(1)}, bf16[256,1,256]{2,0,1:T(8,128)(2,1)}, u32[]{:S(2)}) copy-start(bf16[256,1,256]{2,0,1:T(8,128)(2,1)} %param.16) | copy-start | bytes 393220
  186.4 0.6 copy-start.7
  188.8 0.6 copy-start.6
  194.6 231.8 %reduce-scatter.5.cloned.1.call-start = ((), (), s32[]{:S(2)}) async-start(), calls=%async_computation.4 | async-start | bytes 17825792 | tf_op jit(solution)/shard_map/reduce_scatter | solution.py:135
  265.1 32.5 %copy-start.10 = (f32[256,16]{0,1:T(8,128)S(1)}, f32[256,16]{0,1:T(8,128)}, u32[]{:S(2)}) copy-start(f32[256,16]{0,1:T(8,128)} %copy-done.9) | copy-start | bytes 49156
  316.0 151.1 %reduce-scatter.3.cloned.1.call-start = ((), (), s32[]{:S(2)}) async-start(), calls=%async_computation.3 | async-start | bytes 4718592 | tf_op jit(solution)/shard_map/reduce_scatter | solution.py:112
Sparse Core Ops, SparseCore 0:
  79.4 70.2 all-gather.6
  194.8 70.3 all-gather.4
  316.2 110.1 reduce-scatter.4
  429.2 37.8 reduce-scatter.2
